TPU v7x, 512 devices: a whole 4x8x8 slice. The times are simulated.
512 devices in a mesh: row: 16 (over z, core), col: 32 (over x, y).
Axes of the slice: x: 4, y: 8, z: 8, core: 2. Of those that a mesh axis runs over, the one named last changes fastest.
Arguments:
- strip: float32 [20480, 128], P('row'), may hold values from -6 to 6
- block_below: float32 [64, 64], replicated, may hold values from -1 to 1
- inverse_first: float32 [64, 64], replicated, may hold values from -0.5 to 1.5, as said below
- inverse_second: float32 [64, 64], replicated, may hold values from -0.5 to 1.5, as said below
- cotangent: float32 [20480, 20480], P('row', 'col'), may hold values from -0.0390625 to 0.0390625
Outputs:
- strip_grad: float32 [20480, 128], P('row')
Inputs may be any that keep to these rules, and one draw needn't show every extreme that they name: inverse_first is lower triangular with its diagonal in 0.5 to 1.5. inverse_second is lower triangular with its diagonal in 0.5 to 1.5.
All inputs are finite; a program needn't handle non-finite values.
Results may differ from a plain program's by a relative error of at most 0.00007.
Values sent between devices are 32-bit elements; how exact they have to be, the bound alone decides.
A program may use at most 64 MiB of HBM per device.

v0:
```python
import jax
import jax.numpy as jnp
from jax import lax
from jax.sharding import PartitionSpec as P


def from_root(value, axis, source):
    kept = jnp.where(lax.axis_index(axis) == source, value, 0).astype(value.dtype)
    return lax.psum(kept, axis)


def mul(left, right):
    return jnp.dot(left, right, precision=lax.Precision.HIGHEST, preferred_element_type=jnp.float32)


def finish(bar_sum, left_block, inverse_first, inverse_second, panel):
    bar_updated = mul(-bar_sum[:, panel:], inverse_second)
    bar_first = -bar_sum[:, :panel] - mul(bar_updated, left_block)
    return jnp.concatenate([mul(bar_first, inverse_first), bar_updated], axis=1)


def shards(strip, block_below, inverse_first, inverse_second, cotangent):
    panel = inverse_first.shape[0]
    cols_here = cotangent.shape[1]
    ratio = lax.axis_size("col") // lax.axis_size("row")
    col_id = lax.axis_index("col")
    owner = col_id // ratio
    offset = col_id % ratio * cols_here
    lower_first = mul(strip[:, :panel], inverse_first.T)
    left_block = mul(block_below, inverse_first.T)
    updated = strip[:, panel:] - mul(lower_first, left_block.T)
    col_first = from_root(lax.dynamic_slice_in_dim(lower_first, offset, cols_here, 0), "row", owner)
    lower_second = mul(updated, inverse_second.T)
    col_second = from_root(
        lax.dynamic_slice_in_dim(lower_second, offset, cols_here, 0), "row", owner
    )
    col_lower = jnp.concatenate([col_first, col_second], axis=1)
    lower = jnp.concatenate([lower_first, lower_second], axis=1)
    transposed = lax.dot_general(
        cotangent,
        lower,
        (((0,), (0,)), ((), ())),
        precision=lax.Precision.HIGHEST,
        preferred_element_type=jnp.float32,
    )
    col_total = lax.psum(transposed, "row")
    row_index = lax.axis_index("row")
    pieces = []
    for member in range(ratio):
        pieces.append(from_root(col_total, "col", row_index * ratio + member))
    routed = jnp.concatenate(pieces, axis=0)
    local_sum = mul(cotangent, col_lower)
    row_total = lax.psum(local_sum, "col")
    row_total = row_total + routed
    return finish(row_total, left_block, inverse_first, inverse_second, panel)


def solution(mesh):
    return jax.shard_map(
        shards,
        mesh=mesh,
        in_specs=(P("row", None), P(), P(), P(), P("row", "col")),
        out_specs=P("row", None),
        check_vma=False,
    )
```

profile of v0, /device:TPU:64, one launch (start us, length us, event | category | flops | bytes accessed | tf_op | source)
XLA Modules:
  0.0 320.7 jit_solution(9730919756724847951)
XLA Ops:
  6.5 0.0 copy-start
  6.5 0.0 all-reduce.7.cloned.1.call-start
  6.5 1.1 fusion.11
  7.7 2.7 fusion.3
  10.3 2.5 convolution_subtract_fusion
  12.8 1.6 fusion.12
  14.5 0.0 copy-done
  14.5 3.8 %convolution_bitcast_fusion.1 = f32[640,128]{0,1:T(8,128)} fusion(f32[1280,640]{1,0:T(8,128)S(1)} %copy-done, f32[1280,64]{0,1:T(8,128)S(1)} %fusion.12, f32[1280,64]{0,1:T(8,128)} %fusion.3), kind=kOutput, calls=%fused_computation.3 | convolution fusion | flops 1258455040 | bytes 4259840 | tf_op jit(solution)/shard_map/dot_general | solution.py:39
  18.3 0.0 copy-done.1
  18.3 0.7 dynamic-slice_select_fusion
  19.1 0.0 all-reduce.7.cloned.1.call-update
  19.1 0.0 all-reduce.5.cloned.1.call-start
  19.1 118.0 %all-reduce.7.cloned.1.call-done = (f32[640,64]{0,1:T(8,128)}, f32[640,64]{0,1:T(8,128)}, f32[640,128]{0,1:T(8,128)}) async-done(((f32[640,64]{0,1:T(8,128)}, f32[640,64]{0,1:T(8,128)}, f32[640,128]{0,1:T(8,128)}), (f32[640,64]{0,1:T(8,128)}, f32[640,64]{0,1:T(8,128)}, f32[640,128]{0,1:T(8,128)})) %all-reduce.7.cloned.1.call-update) | async-done | bytes 655376 | tf_op jit(solution)/shard_map/psum | solution.py:9
  137.2 5.3 %convolution_bitcast_fusion = f32[1280,128]{0,1:T(8,128)} fusion(f32[1280,640]{1,0:T(8,128)S(1)} %copy-done, f32[640,64]{0,1:T(8,128)} %get-tuple-element.8, f32[640,64]{0,1:T(8,128)} %get-tuple-element.9), kind=kOutput, calls=%fused_computation.1 | convolution fusion | flops 1258373120 | bytes 4259840 | tf_op jit(solution)/shard_map/dot_general | solution.py:13
  142.5 0.0 copy-done.2
  142.5 0.9 broadcast_select_fusion.1
  143.4 0.0 all-reduce.5.cloned.1.call-update
  143.4 164.6 %all-reduce.5.cloned.1.call-done = (f32[1280,128]{0,1:T(8,128)}, f32[640,128]{0,1:T(8,128)}, f32[640,128]{0,1:T(8,128)}) async-done(((f32[1280,128]{0,1:T(8,128)}, f32[640,128]{0,1:T(8,128)}, f32[640,128]{0,1:T(8,128)}), (f32[1280,128]{0,1:T(8,128)}, f32[640,128]{0,1:T(8,128)}, f32[640,128]{0,1:T(8,128)})) %all-reduce.5.cloned.1.call-update) | async-done | bytes 1310736 | tf_op jit(solution)/shard_map/psum | solution.py:53
  308.0 1.3 maximum_add_fusion
  309.4 0.5 fusion.5
  309.8 0.5 convolution_subtract_fusion.1
  310.3 0.5 fusion.13
  310.8 0.9 pad_maximum_fusion
  311.7 2.2 copy.6
  (6 shorter events, 0.0 us)
Async XLA Ops:
  6.5 7.9 %copy-start = (f32[1280,640]{1,0:T(8,128)S(1)}, f32[1280,640]{1,0:T(8,128)}, u32[]{:S(2)}) copy-start(f32[1280,640]{1,0:T(8,128)} %param.9) | copy-start | bytes 9830404
  6.5 130.6 %all-reduce.7.cloned.1.call-start = ((), (), s32[]{:S(2)}) async-start(), calls=%async_computation.1 | async-start | bytes 1310720 | tf_op jit(solution)/shard_map/psum | solution.py:9
  10.3 8.0 %copy-start.1 = (f32[1280,64]{0,1:T(8,128)S(1)}, f32[1280,64]{0,1:T(8,128)}, u32[]{:S(2)}) copy-start(f32[1280,64]{0,1:T(8,128)} %fusion.3) | copy-start | bytes 983044
  19.1 288.9 %all-reduce.5.cloned.1.call-start = ((), (), s32[]{:S(2)}) async-start(), calls=%async_computation | async-start | bytes 2621440 | tf_op jit(solution)/shard_map/psum | solution.py:53
  137.2 5.3 %copy-start.2 = (f32[640,128]{0,1:T(8,128)S(1)}, f32[640,128]{0,1:T(8,128)}, u32[]{:S(2)}) copy-start(f32[640,128]{0,1:T(8,128)} %get-tuple-element.10) | copy-start | bytes 983044
  137.2 172.2 %copy-start.4 = (f32[64,64]{1,0:T(8,128)S(1)}, f32[64,64]{1,0:T(8,128)}, u32[]{:S(2)}) copy-start(f32[64,64]{1,0:T(8,128)} %param.8) | copy-start | bytes 49156
  142.5 167.8 %copy-start.3 = (f32[64,64]{1,0:T(8,128)S(1)}, f32[64,64]{1,0:T(8,128)}, u32[]{:S(2)}) copy-start(f32[64,64]{1,0:T(8,128)} %param.7) | copy-start | bytes 49156
Sparse Core Ops, SparseCore 0:
  19.2 117.9 all-reduce.6
  143.5 164.4 all-reduce.4
where the time goes:
time: 321 us
  waiting for transfers between devices  283 us (88%)
  matrix products  18.5 us (6%)
  between operations  13.5 us (4%)
  other arithmetic  3.85 us (1%)
    psum x1, waiting for transfers between devices, shards(): row_total = lax.psum(local_sum, 'col')  165 us
    psum x1, waiting for transfers between devices, from_root(): return lax.psum(kept, axis)  118 us
    dot_general x8, matrix products, mul(): jnp.dot(left, right, precision=lax.Precision.HIGHEST, preferred_element_t...  14.6 us
  transfers between devices with their start and end apart: 2, of which 2 were waited for; matrix products, arithmetic and copies ran while one was open for 0% of the time, Pallas kernels for 0%

commit v1 on v0

--- a/solution.py
+++ b/solution.py
@@ -4,9 +4,15 @@
 from jax.sharding import PartitionSpec as P
 
 
+def summed_here(array, axis):
+    parts = lax.all_gather(array, axis, axis=0, tiled=False)
+    summed = parts.sum(axis=0)
+    return summed
+
+
 def from_root(value, axis, source):
     kept = jnp.where(lax.axis_index(axis) == source, value, 0).astype(value.dtype)
-    return lax.psum(kept, axis)
+    return summed_here(kept, axis)
 
 
 def mul(left, right):

time: 321 us -> 629 us (1.96)
  waiting for transfers between devices: 283 us -> 551 us
  local copies, waits for them, and re-layouts: 2.18 us -> 28.5 us
  other arithmetic: 3.85 us -> 19.5 us
    all_gather x0 -> x4, waiting for transfers between devices: none -> 299 us  [summed_here(): parts = lax.all_gather(array, axis, axis=0, tiled=False)]
    unnamed x10 -> x16, local copies, waits for them, and re-layouts: 0.02 us -> 26.3 us
    psum x1, waiting for transfers between devices: 165 us -> 139 us  [shards(): row_total = lax.psum(local_sum, 'col')]
    reduce_sum x0 -> x2, other arithmetic: none -> 12.2 us  [summed_here(): summed = parts.sum(axis=0)]
  transfers between devices with their start and end apart: 2 -> 6, of which waited for: 2 -> 6; matrix products, arithmetic and copies ran while one was open for 0% -> 7% of each run, Pallas kernels for 0% -> 0%
where the time goes in v1:
time: 629 us
  waiting for transfers between devices  551 us (88%)
  local copies, waits for them, and re-layouts  28.5 us (5%)
  other arithmetic  19.5 us (3%)
  matrix products  15.7 us (2%)
  between operations  13.6 us (2%)
    all_gather x4, waiting for transfers between devices, summed_here(): parts = lax.all_gather(array, axis, axis=0, tiled=False)  299 us
    psum x1, waiting for transfers between devices, shards(): row_total = lax.psum(local_sum, 'col')  139 us
    psum x1, waiting for transfers between devices, shards(): col_total = lax.psum(transposed, 'row')  112 us
    unnamed x16, local copies, waits for them, and re-layouts  26.3 us
    dot_general x8, matrix products, mul(): jnp.dot(left, right, precision=lax.Precision.HIGHEST, preferred_element_t...  12.8 us
  transfers between devices with their start and end apart: 6, of which 6 were waited for; matrix products, arithmetic and copies ran while one was open for 7% of the time, Pallas kernels for 0%

profile of v1, /device:TPU:64, one launch (start us, length us, event | category | flops | bytes accessed | tf_op | source)
XLA Modules:
  0.0 628.7 jit_solution(7800177671469841524)
XLA Ops:
  6.5 1.1 fusion.11
  7.7 1.9 fusion.3
  9.6 2.5 convolution_subtract_fusion
  12.1 1.6 fusion.12
  14.4 2.9 convolution_bitcast_fusion.1
  17.4 1.6 dynamic-slice_select_fusion.1
  19.1 1.6 dynamic-slice_select_fusion
  20.8 112.1 %all-reduce.5.cloned.1.call-done = f32[640,128]{0,1:T(8,128)} async-done(((f32[640,128]{0,1:T(8,128)}), f32[640,128]{0,1:T(8,128)}) %all-reduce.5.cloned.1.call-update) | async-done | bytes 327696 | tf_op jit(solution)/shard_map/psum | solution.py:52
  132.8 1.9 broadcast_select_fusion.1
  135.5 43.4 %all-gather.9.cloned.1.call-done = f32[10240,64]{0,1:T(8,128)} async-done(((f32[640,64]{0,1:T(8,128)}), f32[10240,64]{0,1:T(8,128)}) %all-gather.9.cloned.1.call-update) | async-done | bytes 2621456 | tf_op jit(solution)/shard_map/all_gather | solution.py:8
  179.0 3.7 copy.8
  182.7 40.6 %all-gather.11.cloned.1.call-done = f32[10240,64]{0,1:T(8,128)} async-done(((f32[640,64]{0,1:T(8,128)}), f32[10240,64]{0,1:T(8,128)}) %all-gather.11.cloned.1.call-update) | async-done | bytes 2621456 | tf_op jit(solution)/shard_map/all_gather | solution.py:8
  223.3 2.4 copy.9
  225.8 0.9 bitcast_reduce_fusion.2
  226.7 4.3 convolution_bitcast_fusion
  231.0 109.2 %all-gather.13.cloned.1.call-done = f32[20480,128]{0,1:T(8,128)} async-done(((f32[640,128]{0,1:T(8,128)}), f32[20480,128]{0,1:T(8,128)}) %all-gather.13.cloned.1.call-update) | async-done | bytes 10485776 | tf_op jit(solution)/shard_map/all_gather | solution.py:8
  340.2 9.7 %copy.10 = f32[16,8,32,640]{3,2,1,0:T(8,128)} copy(f32[16,8,32,640]{3,1,2,0:T(8,128)} %bitcast.38) | data formatting | bytes 20971520
  349.9 105.7 %all-gather.15.cloned.1.call-done = f32[20480,128]{0,1:T(8,128)} async-done(((f32[640,128]{0,1:T(8,128)}), f32[20480,128]{0,1:T(8,128)}) %all-gather.15.cloned.1.call-update) | async-done | bytes 10485776 | tf_op jit(solution)/shard_map/all_gather | solution.py:8
  455.6 9.6 %copy.11 = f32[16,8,32,640]{3,2,1,0:T(8,128)} copy(f32[16,8,32,640]{3,1,2,0:T(8,128)} %bitcast.39) | data formatting | bytes 20971520
  465.2 11.4 %bitcast_reduce_fusion = (f32[640,128]{0,1:T(8,128)}, f32[640,128]{0,1:T(8,128)}) fusion(f32[16,8,32,640]{3,2,1,0:T(8,128)} %copy.11, f32[16,8,32,640]{3,2,1,0:T(8,128)} %copy.10), kind=kLoop, calls=%fused_computation | loop fusion | flops 5079040 | bytes 21626880 | tf_op jit(solution)/shard_map/reduce_sum | solution.py:9
  476.6 139.4 %all-reduce.3.cloned.1.call-done = f32[1280,128]{0,1:T(8,128)} async-done(((f32[1280,128]{0,1:T(8,128)}), f32[1280,128]{0,1:T(8,128)}) %all-reduce.3.cloned.1.call-update) | async-done | bytes 655376 | tf_op jit(solution)/shard_map/psum | solution.py:59
  616.0 1.3 maximum_add_fusion
  618.8 0.9 pad_maximum_fusion
  619.7 2.2 copy.7
  (27 shorter events, 3.3 us)
Async XLA Ops:
  6.5 7.9 %copy-start = (f32[1280,640]{1,0:T(8,128)S(1)}, f32[1280,640]{1,0:T(8,128)}, u32[]{:S(2)}) copy-start(f32[1280,640]{1,0:T(8,128)} %param.9) | copy-start | bytes 9830404
  6.5 126.3 %all-reduce.5.cloned.1.call-start = ((), (), s32[]{:S(2)}) async-start(), calls=%async_computation.1 | async-start | bytes 655360 | tf_op jit(solution)/shard_map/psum | solution.py:52
  9.6 4.1 copy-start.2
  13.7 0.7 copy-start.3
  17.3 161.7 %all-gather.9.cloned.1.call-start = ((), (), s32[]{:S(2)}) async-start(), calls=%async_computation.2 | async-start | bytes 2785280 | tf_op jit(solution)/shard_map/all_gather | solution.py:8
  19.0 204.3 %all-gather.11.cloned.1.call-start = ((), (), s32[]{:S(2)}) async-start(), calls=%async_computation.3 | async-start | bytes 2785280 | tf_op jit(solution)/shard_map/all_gather | solution.py:8
  20.7 319.5 %all-gather.13.cloned.1.call-start = ((), (), s32[]{:S(2)}) async-start(), calls=%async_computation.4 | async-start | bytes 10813440 | tf_op jit(solution)/shard_map/all_gather | solution.py:8
  134.7 320.9 %all-gather.15.cloned.1.call-start = ((), (), s32[]{:S(2)}) async-start(), calls=%async_computation.5 | async-start | bytes 10813440 | tf_op jit(solution)/shard_map/all_gather | solution.py:8
  135.3 480.7 %all-reduce.3.cloned.1.call-start = ((), (), s32[]{:S(2)}) async-start(), calls=%async_computation | async-start | bytes 1310720 | tf_op jit(solution)/shard_map/psum | solution.py:59
  223.3 2.5 copy-start.1
  465.2 152.1 %copy-start.5 = (f32[64,64]{1,0:T(8,128)S(1)}, f32[64,64]{1,0:T(8,128)}, u32[]{:S(2)}) copy-start(f32[64,64]{1,0:T(8,128)} %param.8) | copy-start | bytes 49156
  476.6 141.7 %copy-start.4 = (f32[64,64]{1,0:T(8,128)S(1)}, f32[64,64]{1,0:T(8,128)}, u32[]{:S(2)}) copy-start(f32[64,64]{1,0:T(8,128)} %param.7) | copy-start | bytes 49156
Sparse Core Ops, SparseCore 0:
  17.4 115.3 all-reduce.4
  135.2 43.7 all-gather.8
  181.3 41.8 all-gather.10
  226.9 113.1 all-gather.12
  343.8 111.7 all-gather.14
  459.2 156.7 all-reduce.2
